TPU v7x, 256 devices: a whole 4x4x8 slice. The times are simulated.
256 devices in a mesh: cp: 32 (over z_lo, y, core), tp: 8 (over z_hi, x).
Axes of the slice: x: 4, y: 4, z: 8 (z_hi: 2, z_lo: 4; z = z_hi * 4 + z_lo), core: 2. Of those that a mesh axis runs over, the one named last changes fastest.
Arguments:
- tokens: bfloat16 [16384, 4096], P('cp', 'tp'), may hold values from -40 to 40
- span_ids: int32 [32, 2], P('cp'), may hold values from 0 to 63, as said below
- positions: int32 [16384], P('cp'), may hold values from 0 to 8191, as said below
- q_weight: bfloat16 [4096, 4096], P(None, 'tp'), may hold values from -0.09375 to 0.09375
- k_weight: bfloat16 [4096, 1024], P(None, 'tp'), may hold values from -0.09375 to 0.09375
- v_weight: bfloat16 [4096, 1024], P(None, 'tp'), may hold values from -0.09375 to 0.09375
- o_weight: bfloat16 [4096, 4096], P('tp'), may hold values from -0.09375 to 0.09375
Outputs:
- attended: bfloat16 [16384, 4096], P('cp', 'tp')
Inputs may be any that keep to these rules, and one draw needn't show every extreme that they name: `span_ids`: row r names the two spans held by index r of cp: a span c and the span 64 - 1 - c, in either order; every span is named once. Span c covers the places c * (256) to (c + 1) * 256 - 1 of the sequence. `positions`: along the sequence (in the order of places given by span_ids) documents are runs of consecutive tokens; a position is 0 at a document's first token and rises by one up to its last, and the first place of the sequence has position 0.
All inputs are finite; a program needn't handle non-finite values.
Results may differ from a plain program's by a relative error of at most 0.014.
The roundings to bfloat16 on the way count: a program that leaves them out, or rounds other values in their place, can miss the bound.
Values may be sent and summed in bfloat16 or wider, within the bound.
A program may use at most 64 MiB of HBM per device.

v0:
```python
import jax
import jax.numpy as jnp
from jax import lax
from jax.experimental import pallas as pl
from jax.experimental.pallas import tpu as pltpu
from jax.sharding import Mesh
from jax.sharding import PartitionSpec as P

HD = 128
SPAN = 256
LOG2E = 1.4426950408889634
TP = ("tp_0", "tp_1")
CP = ("cp_0", "cp_1", "cp_2")


theta_base = 500000.0
floor_score = -1e30


MESH = pl.DeviceIdType.MESH
CHUNKS = 4
ROWS = 128
TAG = 2 * ROWS
BLOCK = TAG + 16


def shifted(x=0, y=0, z=0, row=0, other_core=False):
    place = {}
    if x:
        place["tp_1"] = lax.rem(lax.axis_index("tp_1") + x + 4, 4)
    if y:
        place["cp_1"] = lax.rem(lax.axis_index("cp_1") + y + 4, 4)
    if z:
        place["tp_0"] = 1 - lax.axis_index("tp_0")
    if row:
        place["cp_0"] = lax.rem(lax.axis_index("cp_0") + row + 4, 4)
    if other_core:
        place["cp_2"] = 1 - lax.axis_index("cp_2")
    return place


def greet(peers):
    barrier = pltpu.get_barrier_semaphore()
    for peer in peers:
        pl.semaphore_signal(barrier, inc=1, device_id=peer, device_id_type=MESH)
    pl.semaphore_wait(barrier, len(peers))


def sending(source, target, sems, index, peer, arrival=None):
    return pltpu.make_async_remote_copy(
        src_ref=source,
        dst_ref=target,
        send_sem=sems[0].at[index],
        recv_sem=sems[1].at[index if arrival is None else arrival],
        device_id=peer,
        device_id_type=MESH,
    )


def send(source, target, sems, index, peer):
    copy = sending(source, target, sems, index, peer)
    copy.start()
    return copy


def columns_of(line):
    return jnp.broadcast_to(line, (128, 128)).T


def turn_table(line):
    lane = lax.rem(lax.broadcasted_iota(jnp.int32, (8, 128), 1), HD // 2)
    frequency = jnp.zeros((8, 128), jnp.float32)
    for j in range(HD // 2):
        frequency = jnp.where(lane == j, theta_base ** (-2.0 * j / HD), frequency)
    angle = columns_of(line.astype(jnp.float32)) * frequency[:1]
    turns = jnp.floor(angle * 0.6366197723675814 + 0.5)
    rest = ((angle - turns * 1.5703125) - turns * 4.837512969970703e-4) - turns * 7.549789954891882e-8
    square = rest * rest
    cosine = (2.443315711809948e-5 * square - 1.388731625493765e-3) * square + 4.166664568298827e-2
    cosine = cosine * square * square - 0.5 * square + 1.0
    sine = (-1.9515295891e-4 * square + 8.3321608736e-3) * square - 1.6666654611e-1
    sine = sine * square * rest + rest
    quarter = turns - 4.0 * jnp.floor(turns * 0.25)
    odd = (quarter == 1.0) | (quarter == 3.0)
    cos_all = jnp.where(odd, sine, cosine)
    sin_all = jnp.where(odd, cosine, sine)
    cos_all = jnp.where((quarter == 1.0) | (quarter == 2.0), -cos_all, cos_all)
    sin_all = jnp.where(quarter >= 2.0, -sin_all, sin_all)
    side = lax.broadcasted_iota(jnp.int32, (128, 128), 1)
    return cos_all, jnp.where(side < HD // 2, -sin_all, sin_all)


ORDER = (
    "n0", "a0", "n1", "f0", "a1", "d0", "x0", "n2", "f1", "n3",
    "a2", "d1", "x1", "s0", "f2", "a3", "d2", "x2", "s1", "w0",
    "f3", "d3", "l0", "x3", "s2", "w1", "s3", "w2", "l1", "w3",
    "l2", "l3",
)
TOKEN_SEMS = 9
KEY_SEMS = 20


def project_kernel(
    ids_hbm,
    positions_hbm,
    tokens_hbm,
    wq_hbm,
    wk_hbm,
    wv_hbm,
    q_ref,
    kv_ref,
    ids_ref,
    positions_ref,
    tokens_ref,
    wq_ref,
    wk_ref,
    wv_ref,
    held,
    load_sem,
    token_send,
    token_recv,
    key_send,
    key_recv,
):
    x, zhi = lax.axis_index("tp_1"), lax.axis_index("tp_0")
    row, y, core = lax.axis_index("cp_0"), lax.axis_index("cp_1"), lax.axis_index("cp_2")
    loads = [
        pltpu.make_async_copy(a, b, load_sem.at[i])
        for i, (a, b) in enumerate(
            (
                (tokens_hbm, tokens_ref),
                (ids_hbm, ids_ref),
                (positions_hbm, positions_ref),
                (wk_hbm, wk_ref),
                (wv_hbm, wv_ref),
                (wq_hbm, wq_ref),
            )
        )
    ]
    for load in loads:
        load.start()
    right, left, across = shifted(x=1), shifted(x=-1), shifted(z=1)
    up, down, mate = shifted(y=1), shifted(y=-1), shifted(other_core=True)
    rows_of = [shifted(row=d) for d in (1, 2, 3)]
    greet([right, left, across, up, down, mate] + rows_of)
    tok, key = (token_send, token_recv), (key_send, key_recv)
    sent = []
    half = ROWS // 2
    inner = (row == 1) | (row == 2)
    loads[0].wait()

    def token_rows(c, part=None):
        if part is None:
            return pl.ds(c * ROWS, ROWS)
        return pl.ds(c * ROWS + part * half, half)

    def across_send(c):
        rows = token_rows(c)
        copy = send(
            tokens_ref.at[rows], held.at[1, 0, rows], tok, c * TOKEN_SEMS + 8, across
        )
        sent.append(copy)
        return copy

    def side_sends(c, dz):
        rows = token_rows(c)
        source = held.at[1, 0, rows] if dz else tokens_ref.at[rows]
        a = send(source, held.at[dz, 3, rows], tok, c * TOKEN_SEMS + dz * 4, right)
        b = send(source, held.at[dz, 1, rows], tok, c * TOKEN_SEMS + dz * 4 + 1, left)
        sent.extend((a, b))
        return a, b

    def side_forwards(c, dz):
        at = c * TOKEN_SEMS + dz * 4
        rows = token_rows(c, 0)
        a = send(held.at[dz, 3, rows], held.at[dz, 2, rows], tok, at + 2, right)
        rows = token_rows(c, 1)
        b = send(held.at[dz, 1, rows], held.at[dz, 2, rows], tok, at + 3, left)
        sent.extend((a, b))
        return a, b

    def product(c, dz, dx):
        owner = lax.rem(zhi + dz, 2) * 4 + lax.rem(x + dx, 4)
        rows = pl.ds(pl.multiple_of(owner * 512, 512), 512)
        weights = jnp.concatenate([wk_ref[rows, :], wv_ref[rows, :], wq_ref[rows, :]], axis=1)
        if dz == 0 and dx == 0:
            features = tokens_ref[token_rows(c), :]
        else:
            features = held[dz, dx, token_rows(c), :]
        return jnp.dot(features, weights, preferred_element_type=jnp.float32)

    def key_rows(c):
        at = c * KEY_SEMS
        block = kv_ref.at[c, core, y, row]
        out = []
        for d, skip in ((1, row == 3), (2, None), (3, row == 0)):
            copy = sending(block, block, key, at + d - 1, rows_of[d - 1])
            if skip is None:
                copy.start()
            else:
                pl.when(jnp.logical_not(skip))(copy.start)
            out.append(copy)
        return out, [key_side(c, 0)]

    def key_side(c, d):
        block = kv_ref.at[c, core, y, lax.rem(row + 4 - d, 4)]
        a = send(block, block, key, c * KEY_SEMS + 4 + d, up)
        b = send(block, block, key, c * KEY_SEMS + 8 + d, down)
        sent.extend((a, b))
        return a, b

    def key_relay(c):
        at = c * KEY_SEMS
        block = kv_ref.at[c, core, y, lax.rem(row + 2, 4)]
        end = {"cp_0": jnp.where(row == 2, 3, 0)}
        arrival = at + jnp.where(row == 2, 2, 0)
        return sending(block, block, key, at + 3, end, arrival)

    def key_sides(c, started):
        out, sides = started
        relay = key_relay(c)
        out[1].wait_recv()
        pl.when(inner)(relay.start)
        sides.append(key_side(c, 2))
        out[0].wait_recv()
        sides.append(key_side(c, 1))
        out[2].wait_recv()
        sides.append(key_side(c, 3))
        mine = kv_ref.at[c, core, y]
        m = send(mine, mine, key, c * KEY_SEMS + 16, mate)
        sent.append(m)
        return sides, m, relay

    def key_forwards(c, state):
        sides, m, relay = state
        at = c * KEY_SEMS
        behind, ahead = lax.rem(y + 3, 4), lax.rem(y + 1, 4)
        forwards = []
        for place, d in enumerate((0, 2, 1, 3)):
            a, b = sides[place]
            block_at = lax.rem(row + 4 - d, 4)
            a.wait_recv()
            b.wait_recv()
            if d in (0, 1):
                block = kv_ref.at[c, core, behind, block_at]
                f = send(block, block, key, at + 12 + d, up)
            else:
                block = kv_ref.at[c, core, ahead, block_at]
                f = send(block, block, key, at + 12 + d, down)
            forwards.append(f)
        mates = [m]
        for i, at_y in enumerate((behind, ahead)):
            got = kv_ref.at[c, core, at_y]
            mates.append(send(got, got, key, at + 17 + i, mate))
        sent.extend(forwards + mates[1:])
        return forwards, mates

    def key_last(c, moved):
        forwards, mates = moved
        for f in forwards:
            f.wait_recv()
        got = kv_ref.at[c, core, lax.rem(y + 2, 4)]
        mc = send(got, got, key, c * KEY_SEMS + 19, mate)
        sent.append(mc)
        return mates + [mc]

    across_of, own_of, far_of, near_on, far_on = {}, {}, {}, {}, {}
    rows_at, sides_at, moved_at, totals, mates = {}, {}, {}, {}, []

    def near_step(c):
        for copy in own_of[c]:
            copy.wait_recv()
        near_on[c] = side_forwards(c, 0)

    def across_step(c):
        if c < CHUNKS:
            across_of[c].wait_recv()
            far_of[c] = side_sends(c, 1)

    def far_step(c):
        if c < CHUNKS:
            for copy in far_of[c]:
                copy.wait_recv()
            far_on[c] = side_forwards(c, 1)

    def multiply(c):
        total = product(c, 0, 0)
        for dz, dx in ((0, 3), (0, 1), (1, 0), (1, 3), (1, 1)):
            total = total + product(c, dz, dx)
        totals[c] = total

    def finish(c):
        total = totals[c]
        cosine, sine = turn_table(positions_ref[c : c + 1, :])
        for copy in near_on[c]:
            copy.wait_recv()
        total = total + product(c, 0, 2)
        for copy in far_on[c]:
            copy.wait_recv()
        total = total + product(c, 1, 2)

        def turned(vectors):
            return (vectors * cosine + pltpu.roll(vectors, HD // 2, 1) * sine).astype(jnp.bfloat16)

        kv_ref[c, core, y, row, :ROWS, :] = turned(total[:, :HD])
        kv_ref[c, core, y, row, ROWS:TAG, :] = total[:, HD : 2 * HD].astype(jnp.bfloat16)
        tag = ids_ref[0, c // 2].astype(jnp.float32)
        kv_ref[c, core, y, row, TAG:, :] = jnp.full((16, HD), tag, jnp.float32).astype(jnp.bfloat16)
        rows_at[c] = key_rows(c)
        for head in range(4):
            at = head * SPAN + (c % 2) * ROWS
            q_ref[c // 2, at : at + ROWS, :] = turned(total[:, (2 + head) * HD : (3 + head) * HD])

    def side_step(c):
        sides_at[c] = key_sides(c, rows_at[c])

    def forward_step(c):
        moved_at[c] = key_forwards(c, sides_at[c])

    def last_step(c):
        mates.extend(key_last(c, moved_at[c]))

    for c in range(CHUNKS):
        own_of[c] = side_sends(c, 0)
        across_of[c] = across_send(c)
    actions = {
        "n": near_step,
        "a": across_step,
        "f": far_step,
        "d": multiply,
        "x": finish,
        "s": side_step,
        "w": forward_step,
        "l": last_step,
    }
    for action in ORDER:
        if action == "d0":
            for load in loads[1:]:
                load.wait()
        actions[action[0]](int(action[1:]))
    for copy in mates:
        copy.wait_recv()
    for copy in sent:
        copy.wait_send()
    for c in range(CHUNKS):
        out = rows_at[c][0]
        out[1].wait_send()
        pl.when(row != 3)(out[0].wait_send)
        pl.when(row != 0)(out[2].wait_send)
        pl.when(inner)(sides_at[c][2].wait_send)


def project(span_ids, positions, tokens, q_weight, k_weight, v_weight):
    vmem = pl.BlockSpec(memory_space=pltpu.VMEM)
    hbm = pl.BlockSpec(memory_space=pltpu.HBM)
    return pl.pallas_call(
        project_kernel,
        out_shape=(
            jax.ShapeDtypeStruct((2, 4 * SPAN, HD), jnp.bfloat16),
            jax.ShapeDtypeStruct((CHUNKS, 2, 4, 4, BLOCK, HD), jnp.bfloat16),
        ),
        in_specs=[hbm] * 6,
        out_specs=(vmem, vmem),
        scratch_shapes=[
            pltpu.SMEM(span_ids.shape, jnp.int32),
            pltpu.VMEM(positions.shape, jnp.int32),
            pltpu.VMEM(tokens.shape, jnp.bfloat16),
            pltpu.VMEM(q_weight.shape, jnp.bfloat16),
            pltpu.VMEM(k_weight.shape, jnp.bfloat16),
            pltpu.VMEM(v_weight.shape, jnp.bfloat16),
            pltpu.VMEM((2, 4) + tokens.shape, jnp.bfloat16),
            pltpu.SemaphoreType.DMA((6,)),
            pltpu.SemaphoreType.DMA((CHUNKS * TOKEN_SEMS,)),
            pltpu.SemaphoreType.DMA((CHUNKS * TOKEN_SEMS,)),
            pltpu.SemaphoreType.DMA((CHUNKS * KEY_SEMS,)),
            pltpu.SemaphoreType.DMA((CHUNKS * KEY_SEMS,)),
        ],
        compiler_params=pltpu.CompilerParams(
            collective_id=0, has_side_effects=True, vmem_limit_bytes=26 * 1024 * 1024
        ),
        name="project",
    )(
        *(
            pltpu.with_memory_space_constraint(array, pltpu.HBM)
            for array in (span_ids, positions, tokens, q_weight, k_weight, v_weight)
        )
    )


WIDTHS = (4, 2, 1)


def attend_kernel(
    ids_hbm, positions_hbm, q_ref, kv_ref, out_ref, ids, places_of, positions_ref, top_ref, acc_ref,
    start_ref, table_ref, where, sems,
):
    loads = [
        pltpu.make_async_copy(a, b, sems.at[i + 1])
        for i, (a, b) in enumerate(
            ((ids_hbm, ids), (positions_hbm, positions_ref), (positions_hbm, places_of))
        )
    ]
    for load in loads:
        load.start()
    heads = q_ref.shape[1] // SPAN
    scale = LOG2E * HD**-0.5
    ones = jnp.ones((SPAN, HD), jnp.bfloat16)
    lane = lax.broadcasted_iota(jnp.int32, (8, 128), 1).astype(jnp.float32)
    table = jnp.zeros((8, 128), jnp.int32)
    for block in range(64):
        at = (block // 32) * 64 + block % 32
        tag = kv_ref[at, TAG:, :].astype(jnp.float32)[:8]
        table = table + jnp.where(tag == lane, block, 0)
    table_ref[...] = table
    fetch = pltpu.make_async_copy(table_ref, where, sems.at[0])
    fetch.start()
    row, y, core = lax.axis_index("cp_0"), lax.axis_index("cp_1"), lax.axis_index("cp_2")
    home = core * 16 + y * 4 + row
    for load in loads:
        load.wait()
    for half in range(2):
        own = ids[0, half]
        for part in range(2):
            line = 2 * half + part
            column = columns_of(positions_ref[line : line + 1, :].astype(jnp.float32))
            place = own * SPAN + part * 128
            place = place + lax.broadcasted_iota(jnp.int32, (128, 128), 0)
            start_ref[half, part * 128 : (part + 1) * 128, :] = place - column.astype(jnp.int32)

    def block(half, span, places_in, masked, first):
        places = []
        for place in places_in:
            first_place = (place // 32) * 64 + lax.rem(place, 32)
            places += [first_place, first_place + 32]
        wide = 2 * len(places_in)
        keys = jnp.concatenate([kv_ref[at, :ROWS, :] for at in places], axis=0)
        values = jnp.concatenate([kv_ref[at, ROWS:TAG, :] for at in places], axis=0)
        values = jnp.concatenate([values, jnp.concatenate([ones] * len(places_in), axis=0)], axis=1)
        if masked:
            key = span * SPAN + lax.broadcasted_iota(jnp.int32, (SPAN, SPAN), 1)
            start = start_ref[half]
            seen = key >= jnp.concatenate([start, start], axis=1)
            if first:
                query = span * SPAN + lax.broadcasted_iota(jnp.int32, (SPAN, SPAN), 0)
                seen = seen & (key <= query)
        for head in range(heads):
            rows = slice(head * SPAN, (head + 1) * SPAN)
            score = lax.dot_general(
                q_ref[half, rows, :],
                keys,
                (((1,), (1,)), ((), ())),
                preferred_element_type=jnp.float32,
            )
            score = score * scale
            if masked:
                score = jnp.where(seen, score, floor_score)
            top = jnp.max(score, axis=1, keepdims=True)
            if first:
                weight = jnp.exp2(score - top)
                top_ref[half, rows, :] = jnp.broadcast_to(top, (SPAN, HD))
            else:
                before = top_ref[half, rows, :]
                now = jnp.maximum(before, top)
                weight = jnp.exp2(score - jnp.concatenate([now] * wide, axis=1))
                fade = jnp.exp2(before - now)
                top_ref[half, rows, :] = now
            mixed = jnp.dot(
                weight.astype(jnp.bfloat16), values, preferred_element_type=jnp.float32
            )
            if not first:
                mixed = mixed + acc_ref[half, rows, :] * jnp.concatenate([fade, fade], axis=1)
            acc_ref[half, rows, :] = mixed

    for half in range(2):
        block(half, ids[0, half], (home + 32 * half,), True, True)
    fetch.wait()
    for half in range(2):
        own = ids[0, half]
        low = (own * SPAN - places_of[2 * half, 0]) // SPAN
        clear = (own * SPAN + 2 * SPAN - 2 - places_of[2 * half + 1, 127]) // SPAN
        clear = jnp.minimum(clear, own)

        def masked_step(span, carry):
            block(half, span, (where[0, span],), True, False)
            return carry

        def clear_steps(begin, count):
            def step(i, carry):
                at = begin + i * count
                block(half, None, [where[0, at + j] for j in range(count)], False, False)
                return carry

            steps = (own - begin) // count
            lax.fori_loop(0, steps, step, 0)
            return begin + steps * count

        lax.fori_loop(low, clear, masked_step, 0)
        for count in WIDTHS:
            clear = clear_steps(clear, count)
        for head in range(heads):
            rows = slice(head * SPAN, (head + 1) * SPAN)
            mixed = acc_ref[half, rows, :HD] / acc_ref[half, rows, HD:]
            out_ref[half * SPAN : (half + 1) * SPAN, head * HD : (head + 1) * HD] = mixed.astype(
                jnp.bfloat16
            )


def attend(span_ids, positions, queries, held):
    vmem = pl.BlockSpec(memory_space=pltpu.VMEM)
    hbm = pl.BlockSpec(memory_space=pltpu.HBM)
    rows = queries.shape[1]
    heads = rows // SPAN
    return pl.pallas_call(
        attend_kernel,
        out_shape=jax.ShapeDtypeStruct((2 * SPAN, heads * HD), jnp.bfloat16),
        in_specs=[hbm, hbm, vmem, vmem],
        out_specs=vmem,
        scratch_shapes=[
            pltpu.SMEM(span_ids.shape, jnp.int32),
            pltpu.SMEM(positions.shape, jnp.int32),
            pltpu.VMEM(positions.shape, jnp.int32),
            pltpu.VMEM((2, rows, HD), jnp.float32),
            pltpu.VMEM((2, rows, 2 * HD), jnp.float32),
            pltpu.VMEM((2, SPAN, HD), jnp.int32),
            pltpu.VMEM((8, 128), jnp.int32),
            pltpu.SMEM((8, 128), jnp.int32),
            pltpu.SemaphoreType.DMA((4,)),
        ],
        compiler_params=pltpu.CompilerParams(vmem_limit_bytes=20 * 1024 * 1024),
        name="attend",
    )(
        *(pltpu.with_memory_space_constraint(array, pltpu.HBM) for array in (span_ids, positions)),
        queries,
        held,
    )


def combine_kernel(
    attn_ref, weight_ref, out_ref, far_out, far_in, near_out, near_in, over_out, over_in, kept,
    send_sem, recv_sem,
):
    x, zhi = lax.axis_index("tp_1"), lax.axis_index("tp_0")
    right, left, across = shifted(x=1), shifted(x=-1), shifted(z=1)
    greet([right, left, across])
    sems = (send_sem, recv_sem)
    steps = kept.shape[0]
    size = kept.shape[1]
    half = size // 2
    width = out_ref.shape[1]
    sent = []

    def share(c, dx):
        rows = attn_ref[c * size : (c + 1) * size, :]
        terms = []
        for dz in range(2):
            owner = lax.rem(zhi + dz, 2) * 4 + lax.rem(x + dx, 4)
            columns = pl.ds(pl.multiple_of(owner * width, width), width)
            terms.append(
                jnp.dot(rows, weight_ref[:, columns], preferred_element_type=jnp.float32)
            )
        return jnp.concatenate(terms, axis=1)

    def open_step(c):
        far = share(c, 2).astype(jnp.bfloat16)
        far_out[c, 0] = far[:half]
        far_out[c, 1] = far[half:]
        a = send(far_out.at[c, 0], far_in.at[c, 0], sems, c * 7, right)
        b = send(far_out.at[c, 1], far_in.at[c, 1], sems, c * 7 + 1, left)
        to_right, to_left = share(c, 1), share(c, 3)
        near_out[c, 0, 1] = to_right[half:].astype(jnp.bfloat16)
        d = send(near_out.at[c, 0, 1], near_in.at[c, 0, 1], sems, c * 7 + 2, right)
        near_out[c, 1, 0] = to_left[:half].astype(jnp.bfloat16)
        e = send(near_out.at[c, 1, 0], near_in.at[c, 1, 0], sems, c * 7 + 3, left)
        near_out[c, 0, 0] = to_right[:half].astype(jnp.bfloat16)
        near_out[c, 1, 1] = to_left[half:].astype(jnp.bfloat16)
        sent.extend((a, b, d, e))
        return a, b, d, e

    def pass_on(c, opened):
        a, b, d, e = opened
        a.wait_recv()
        near_out[c, 0, 0] = (
            near_out[c, 0, 0].astype(jnp.float32) + far_in[c, 0].astype(jnp.float32)
        ).astype(jnp.bfloat16)
        f = send(near_out.at[c, 0, 0], near_in.at[c, 0, 0], sems, c * 7 + 4, right)
        b.wait_recv()
        near_out[c, 1, 1] = (
            near_out[c, 1, 1].astype(jnp.float32) + far_in[c, 1].astype(jnp.float32)
        ).astype(jnp.bfloat16)
        g = send(near_out.at[c, 1, 1], near_in.at[c, 1, 1], sems, c * 7 + 5, left)
        sent.extend((f, g))
        return d, e, f, g

    def cross(c, passed):
        total = share(c, 0)
        for copy in passed:
            copy.wait_recv()
        for side in range(2):
            both = jnp.concatenate([near_in[c, side, 0], near_in[c, side, 1]], axis=0)
            total = total + both.astype(jnp.float32)
        over_out[c] = total[:, width:].astype(jnp.bfloat16)
        kept[c] = total[:, :width]
        copy = send(over_out.at[c], over_in.at[c], sems, c * 7 + 6, across)
        sent.append(copy)
        return copy

    def close(c, crossed):
        crossed.wait_recv()
        out_ref[c * size : (c + 1) * size, :] = (
            kept[c] + over_in[c].astype(jnp.float32)
        ).astype(jnp.bfloat16)

    opened, passed, crossed = {}, {}, {}
    for c in range(2):
        opened[c] = open_step(c)
    for c in range(steps):
        passed[c] = pass_on(c, opened[c])
        if c + 2 < steps:
            opened[c + 2] = open_step(c + 2)
        if c >= 1:
            crossed[c - 1] = cross(c - 1, passed[c - 1])
        if c >= 2:
            close(c - 2, crossed[c - 2])
    crossed[steps - 1] = cross(steps - 1, passed[steps - 1])
    close(steps - 2, crossed[steps - 2])
    close(steps - 1, crossed[steps - 1])
    for copy in sent:
        copy.wait_send()


STEPS = 4


def combine(attention, o_weight):
    vmem = pl.BlockSpec(memory_space=pltpu.VMEM)
    rows, width = attention.shape[0], o_weight.shape[1] // 8
    size = rows // STEPS
    half = (size // 2, 2 * width)
    return pl.pallas_call(
        combine_kernel,
        out_shape=jax.ShapeDtypeStruct((rows, width), jnp.bfloat16),
        in_specs=[vmem, vmem],
        out_specs=vmem,
        scratch_shapes=[
            pltpu.VMEM((STEPS, 2) + half, jnp.bfloat16),
            pltpu.VMEM((STEPS, 2) + half, jnp.bfloat16),
            pltpu.VMEM((STEPS, 2, 2) + half, jnp.bfloat16),
            pltpu.VMEM((STEPS, 2, 2) + half, jnp.bfloat16),
            pltpu.VMEM((STEPS, size, width), jnp.bfloat16),
            pltpu.VMEM((STEPS, size, width), jnp.bfloat16),
            pltpu.VMEM((STEPS, size, width), jnp.float32),
            pltpu.SemaphoreType.DMA((STEPS * 7,)),
            pltpu.SemaphoreType.DMA((STEPS * 7,)),
        ],
        compiler_params=pltpu.CompilerParams(
            collective_id=1, has_side_effects=True, vmem_limit_bytes=32 * 1024 * 1024
        ),
        name="combine",
    )(attention, o_weight)


def per_device(tokens, span_ids, positions, q_weight, k_weight, v_weight, o_weight):
    lines = positions.reshape(CHUNKS, ROWS)
    queries, held = project(span_ids, lines, tokens, q_weight, k_weight, v_weight)
    attention = attend(span_ids, lines, queries, held.reshape(-1, BLOCK, HD))
    return combine(attention, o_weight)


def solution(mesh):
    split = Mesh(mesh.devices.reshape(4, 4, 2, 2, 4), ("cp_0", "cp_1", "cp_2", "tp_0", "tp_1"))
    placed = (P(CP, TP), P(CP, None), P(CP), P(None, TP), P(None, TP), P(None, TP), P(TP, None))
    return jax.shard_map(
        per_device, mesh=split, in_specs=placed, out_specs=P(CP, TP), check_vma=False
    )
```

profile of v0, /device:TPU:16, one launch (start us, length us, event | category | flops | bytes accessed | tf_op | source)
XLA Modules:
  0.0 146.3 jit_solution(6104354060723831586)
XLA Ops:
  0.0 79.6 %project.1 = (bf16[2,1024,128]{2,1,0:T(8,128)(2,1)S(1)}, bf16[4,2,4,4,272,128]{5,4,3,2,1,0:T(8,128)(2,1)S(1)}) custom-call(s32[1,2]{1,0:T(1,128)} %ids_hbm.3, s32[4,128]{1,0:T(4,128)} %bitcast.3, bf16[512,512]{1,0:T(8,128)(2,1)} %tokens_hbm.1, bf16[4096,512]{1,0:T(8,128)(2,1)} %wq_hbm.1, bf16[4096,128]{1,0:T(8,128)(2,1)} %wk_hbm.1, bf16[4096,128]{1,0:T(8,128)(2,1)} %wv_hbm.1), custom_call_target="tpu_custom_call" | custom-call | tf_op jit(solution)/shard_map/project/pallas_call | solution.py:356
  79.6 0.0 copy-start
  79.7 16.9 %attend.1.attn_ref = bf16[512,512]{1,0:T(8,128)(2,1)S(1)} custom-call(s32[1,2]{1,0:T(1,128)} %ids_hbm.3, s32[4,128]{1,0:T(4,128)} %bitcast.4, bf16[2,1024,128]{2,1,0:T(8,128)(2,1)S(1)} %get-tuple-element.7.q_ref, bf16[128,272,128]{2,1,0:T(8,128)(2,1)S(1)} %bitcast.2), custom_call_target="tpu_custom_call" | custom-call | tf_op jit(solution)/shard_map/attend/pallas_call | solution.py:513
  96.5 0.0 copy-done
  96.5 48.9 %combine.1 = bf16[512,512]{1,0:T(8,128)(2,1)S(1)} custom-call(bf16[512,512]{1,0:T(8,128)(2,1)S(1)} %attend.1.attn_ref, bf16[512,4096]{1,0:T(8,128)(2,1)S(1)} %copy-done), custom_call_target="tpu_custom_call" | custom-call | tf_op jit(solution)/shard_map/combine/pallas_call | solution.py:639
  145.5 0.8 copy.9
Async XLA Ops:
  79.6 16.9 %copy-start = (bf16[512,4096]{1,0:T(8,128)(2,1)S(1)}, bf16[512,4096]{1,0:T(8,128)(2,1)}, u32[]{:S(2)}) copy-start(bf16[512,4096]{1,0:T(8,128)(2,1)} %weight_ref.1) | copy-start | bytes 12582916
where the time goes:
time: 148 us; the launch traced here: 146 us
  Pallas kernels  145 us (98%)
    pallas_call x1, Pallas kernels, project(): pl.pallas_call(project_kernel, out_shape=(jax.ShapeDtypeStruct((2, 4 * SP...  79.6 us
    pallas_call x1, Pallas kernels, combine(): pl.pallas_call(combine_kernel, out_shape=jax.ShapeDtypeStruct((rows, widt...  48.9 us
    pallas_call x1, Pallas kernels, attend(): pl.pallas_call(attend_kernel, out_shape=jax.ShapeDtypeStruct((2 * SPAN, h...  16.9 us

commit v1 on v0

--- a/solution.py
+++ b/solution.py
@@ -535,6 +535,15 @@
     )
 
 
+STEPS = 8
+COMBINE_ORDER = (
+    "o0", "o1", "o2", "o3", "p0", "o4", "p1", "c0", "o5", "p2",
+    "c1", "o6", "p3", "c2", "o7", "p4", "c3", "e0", "p5", "c4",
+    "e1", "p6", "c5", "e2", "p7", "c6", "e3", "c7", "e4", "e5",
+    "e6", "e7",
+)
+
+
 def combine_kernel(
     attn_ref, weight_ref, out_ref, far_out, far_in, near_out, near_in, over_out, over_in, kept,
     send_sem, recv_sem,
@@ -611,24 +620,18 @@
         ).astype(jnp.bfloat16)
 
     opened, passed, crossed = {}, {}, {}
-    for c in range(2):
-        opened[c] = open_step(c)
-    for c in range(steps):
-        passed[c] = pass_on(c, opened[c])
-        if c + 2 < steps:
-            opened[c + 2] = open_step(c + 2)
-        if c >= 1:
-            crossed[c - 1] = cross(c - 1, passed[c - 1])
-        if c >= 2:
-            close(c - 2, crossed[c - 2])
-    crossed[steps - 1] = cross(steps - 1, passed[steps - 1])
-    close(steps - 2, crossed[steps - 2])
-    close(steps - 1, crossed[steps - 1])
+    for action in COMBINE_ORDER:
+        c = int(action[1])
+        if action[0] == "o":
+            opened[c] = open_step(c)
+        elif action[0] == "p":
+            passed[c] = pass_on(c, opened[c])
+        elif action[0] == "c":
+            crossed[c] = cross(c, passed[c])
+        else:
+            close(c, crossed[c])
     for copy in sent:
         copy.wait_send()
-
-
-STEPS = 4
 
 
 def combine(attention, o_weight):

time: 148 us -> 146 us (0.986)
  no operation moved by 1% of the time
where the time goes in v1:
time: 146 us; the launch traced here: 145 us
  Pallas kernels  144 us (99%)
    pallas_call x1, Pallas kernels, project(): pl.pallas_call(project_kernel, out_shape=(jax.ShapeDtypeStruct((2, 4 * SP...  79.6 us
    pallas_call x1, Pallas kernels, combine(): pl.pallas_call(combine_kernel, out_shape=jax.ShapeDtypeStruct((rows, widt...  47.8 us
    pallas_call x1, Pallas kernels, attend(): pl.pallas_call(attend_kernel, out_shape=jax.ShapeDtypeStruct((2 * SPAN, h...  16.9 us

profile of v1, /device:TPU:16, one launch (start us, length us, event | category | flops | bytes accessed | tf_op | source)
XLA Modules:
  0.0 145.2 jit_solution(18343882415563549225)
XLA Ops:
  0.0 79.6 %project.1 = (bf16[2,1024,128]{2,1,0:T(8,128)(2,1)S(1)}, bf16[4,2,4,4,272,128]{5,4,3,2,1,0:T(8,128)(2,1)S(1)}) custom-call(s32[1,2]{1,0:T(1,128)} %ids_hbm.3, s32[4,128]{1,0:T(4,128)} %bitcast.3, bf16[512,512]{1,0:T(8,128)(2,1)} %tokens_hbm.1, bf16[4096,512]{1,0:T(8,128)(2,1)} %wq_hbm.1, bf16[4096,128]{1,0:T(8,128)(2,1)} %wk_hbm.1, bf16[4096,128]{1,0:T(8,128)(2,1)} %wv_hbm.1), custom_call_target="tpu_custom_call" | custom-call | tf_op jit(solution)/shard_map/project/pallas_call | solution.py:356
  79.6 0.0 copy-start
  79.7 16.9 %attend.1.attn_ref = bf16[512,512]{1,0:T(8,128)(2,1)S(1)} custom-call(s32[1,2]{1,0:T(1,128)} %ids_hbm.3, s32[4,128]{1,0:T(4,128)} %bitcast.4, bf16[2,1024,128]{2,1,0:T(8,128)(2,1)S(1)} %get-tuple-element.7.q_ref, bf16[128,272,128]{2,1,0:T(8,128)(2,1)S(1)} %bitcast.2), custom_call_target="tpu_custom_call" | custom-call | tf_op jit(solution)/shard_map/attend/pallas_call | solution.py:513
  96.6 0.0 copy-done
  96.6 47.8 %combine.1 = bf16[512,512]{1,0:T(8,128)(2,1)S(1)} custom-call(bf16[512,512]{1,0:T(8,128)(2,1)S(1)} %attend.1.attn_ref, bf16[512,4096]{1,0:T(8,128)(2,1)S(1)} %copy-done), custom_call_target="tpu_custom_call" | custom-call | tf_op jit(solution)/shard_map/combine/pallas_call | solution.py:642
  144.4 0.8 copy.9
Async XLA Ops:
  79.6 16.9 %copy-start = (bf16[512,4096]{1,0:T(8,128)(2,1)S(1)}, bf16[512,4096]{1,0:T(8,128)(2,1)}, u32[]{:S(2)}) copy-start(bf16[512,4096]{1,0:T(8,128)(2,1)} %weight_ref.1) | copy-start | bytes 12582916
